TPU v7x, 32 devices: a whole 2x2x4 slice. The times are simulated.
32 devices in a mesh: rows: 8 (over z, x), wide: 4 (over y, core).
Axes of the slice: x: 2, y: 2, z: 4, core: 2. Of those that a mesh axis runs over, the one named last changes fastest.
Arguments:
- hidden_in: bfloat16 [1024, 16, 1024], P('wide', 'rows'), may hold values from -6 to 6
- segments: int32 [16, 1024], P('rows'), may hold values from 0 to 3, never falling along the last dimension, each value on 1 to 768 neighbouring positions
- prefix_vis: int32 [16, 64], P('rows'), may hold values 0 or 1
- prefix_key: bfloat16 [64, 1024], replicated, may hold values from -6 to 6
- prefix_value: bfloat16 [64, 1024], replicated, may hold values from -6 to 6
- w_query: bfloat16 [1024, 1024], replicated, may hold values from -0.375 to 0.375
- w_key: bfloat16 [1024, 1024], replicated, may hold values from -0.1875 to 0.1875
- w_value: bfloat16 [1024, 1024], replicated, may hold values from -0.1875 to 0.1875
- w_out: bfloat16 [1024, 1024], replicated, may hold values from -4 to 4
- norm1_gain: float32 [1024], replicated, may hold values from 0.1 to 1.9
- norm1_bias: float32 [1024], replicated, may hold values from -3 to 3
- w_up: bfloat16 [1024, 4096], P(None, 'wide'), may hold values from -0.1875 to 0.1875
- w_down: bfloat16 [4096, 1024], P('wide'), may hold values from -0.09375 to 0.09375
- norm2_gain: float32 [1024], replicated, may hold values from 0.1 to 1.9
- norm2_bias: float32 [1024], replicated, may hold values from -3 to 3
- out_grad: float32 [1024, 16, 1024], P('wide', 'rows'), may hold values from -6 to 6
Outputs:
- block_out: bfloat16 [1024, 16, 1024], P('wide', 'rows')
- input_grad: float32 [1024, 16, 1024], P('wide', 'rows')
- prefix_key_grad: float32 [64, 1024], replicated
- prefix_value_grad: float32 [64, 1024], replicated
Inputs may be any that keep to these rules, and one draw needn't show every extreme that they name: `segments`: in each row the segment ids never fall, and a segment holds at most 768 positions.
All inputs are finite; a program needn't handle non-finite values. No bound on the sum of `prefix_vis` on one device may be relied on, other than what follows from the above.
Results may differ from a plain program's by a relative error of at most 0.014.
The roundings to bfloat16 on the way count: a program that leaves them out, or rounds other values in their place, can miss the bound.
Values may be sent and summed in bfloat16 or wider, within the bound.
A program may use at most 256 MiB of HBM per device.

v0:
```python
import jax
import jax.numpy as jnp
from jax import lax
from jax.sharding import PartitionSpec as P

H = 16
E = 64
P_SIZE = 64
norm_eps = 1e-05
neg_large = -1e30
root_half = 0.7071067811865476
inv_root_tau = 0.3989422804014327


def norm_forward(summed, norm_gain, norm_bias):
    average = jnp.mean(summed, axis=-1, keepdims=True)
    centred = summed - average
    variance = jnp.mean(centred * centred, axis=-1, keepdims=True)
    inv_std = lax.rsqrt(variance + norm_eps)
    scaled = centred * inv_std
    return (scaled * norm_gain + norm_bias, scaled, inv_std)


def norm_backward(grad_out, scaled, inv_std, norm_gain):
    shaped = grad_out * norm_gain
    return inv_std * (
        shaped
        - jnp.mean(shaped, axis=-1, keepdims=True)
        - scaled * jnp.mean(shaped * scaled, axis=-1, keepdims=True)
    )


def gelu_slope(hidden_pre):
    return (
        0.5 * (1.0 + lax.erf(hidden_pre * root_half))
        + hidden_pre * jnp.exp(-0.5 * hidden_pre * hidden_pre) * inv_root_tau
    )


def project(left, weight):
    return jnp.einsum("crd,de->cre", left, weight, preferred_element_type=jnp.float32)


def project_back(left, weight):
    return jnp.einsum("cre,de->crd", left, weight, preferred_element_type=jnp.float32)


def heads_of(block, model_width, first):
    picked = block[..., first * model_width : (first + 1) * model_width]
    return picked.reshape(block.shape[0], block.shape[1], H, E)


def attention_probs(query_heads, key_heads, own_seg, all_seg, prefix_vis, prefix_keys):
    seq_scores = jnp.einsum(
        "crhe,lrhe->rhcl", query_heads, key_heads, preferred_element_type=jnp.float32
    )
    pre_scores = jnp.einsum(
        "crhe,phe->rhcp", query_heads, prefix_keys, preferred_element_type=jnp.float32
    )
    same_seg = (own_seg[:, :, None] == all_seg[:, None, :])[:, None]
    visible = (prefix_vis > 0)[:, None, None, :]
    seq_scores = jnp.where(same_seg, seq_scores, neg_large)
    pre_scores = jnp.where(visible, pre_scores, neg_large)
    row_max = jnp.maximum(jnp.max(seq_scores, axis=-1), jnp.max(pre_scores, axis=-1))[..., None]
    seq_exp = jnp.exp(seq_scores - row_max)
    pre_exp = jnp.exp(pre_scores - row_max)
    prob_total = (jnp.sum(seq_exp, axis=-1) + jnp.sum(pre_exp, axis=-1))[..., None]
    seq_prob = seq_exp / prob_total
    pre_prob = pre_exp / prob_total
    return (
        seq_prob,
        pre_prob,
        seq_prob.astype(jnp.bfloat16),
        pre_prob.astype(jnp.bfloat16),
        row_max,
        prob_total,
    )


def on_device(
    hidden_in,
    segments,
    prefix_vis,
    prefix_key,
    prefix_value,
    w_query,
    w_key,
    w_value,
    w_out,
    norm1_gain,
    norm1_bias,
    w_up,
    w_down,
    norm2_gain,
    norm2_bias,
    out_grad,
):
    per_dev = hidden_in.shape[0]
    row_count = hidden_in.shape[1]
    model_width = hidden_in.shape[2]
    offset = lax.axis_index("wide") * per_dev
    own_seg = lax.dynamic_slice_in_dim(segments, offset, per_dev, 1)
    prefix_keys = prefix_key.reshape(P_SIZE, H, E)
    prefix_vals = prefix_value.reshape(P_SIZE, H, E)
    queries = (project(hidden_in, w_query) * 0.125).astype(jnp.bfloat16)
    key_own = project(hidden_in, w_key).astype(jnp.bfloat16)
    value_own = project(hidden_in, w_value).astype(jnp.bfloat16)
    pair_own = jnp.concatenate([key_own, value_own], axis=2)
    pair_all = lax.all_gather(pair_own, "wide", axis=0, tiled=True)
    query_heads = queries.reshape(per_dev, row_count, H, E)
    forward_probs = attention_probs(
        query_heads, heads_of(pair_all, model_width, 0), own_seg, segments, prefix_vis, prefix_keys
    )
    seq_prob, pre_prob, seq_low, pre_low, row_max, prob_total = forward_probs
    mixture = jnp.einsum(
        "rhcl,lrhe->crhe",
        seq_low,
        heads_of(pair_all, model_width, 1),
        preferred_element_type=jnp.float32,
    )
    mixture = mixture + jnp.einsum(
        "rhcp,phe->crhe", pre_low, prefix_vals, preferred_element_type=jnp.float32
    )
    mix_low = mixture.reshape(per_dev, row_count, model_width).astype(jnp.bfloat16)
    attn_out = project(mix_low, w_out)
    normed_one, scaled_one, inv_one = norm_forward(
        hidden_in.astype(jnp.float32) + attn_out, norm1_gain, norm1_bias
    )
    normed_low = normed_one.astype(jnp.bfloat16)

    def up_rows(row_piece):
        return jnp.einsum("lrd,df->lrf", row_piece, w_up, preferred_element_type=jnp.float32)

    hidden_pre = up_rows(lax.all_gather(normed_low, "wide", axis=0, tiled=True))
    hidden_act = jax.nn.gelu(hidden_pre, approximate=False).astype(jnp.bfloat16)
    ffn_out = lax.psum_scatter(
        jnp.einsum("lrf,fd->lrd", hidden_act, w_down, preferred_element_type=jnp.float32),
        "wide",
        scatter_dimension=0,
        tiled=True,
    )
    normed_two, scaled_two, inv_two = norm_forward(normed_one + ffn_out, norm2_gain, norm2_bias)
    block_out = normed_two.astype(jnp.bfloat16)
    grad_two = norm_backward(out_grad, scaled_two, inv_two, norm2_gain)
    grad_ffn = grad_two.astype(jnp.bfloat16)
    pre_back = up_rows(lax.all_gather(normed_low, "wide", axis=0, tiled=True))
    hidden_grad = jnp.einsum(
        "lrd,fd->lrf",
        lax.all_gather(grad_ffn, "wide", axis=0, tiled=True),
        w_down,
        preferred_element_type=jnp.float32,
    )
    pre_rows = pre_back
    grad_pre = (hidden_grad * gelu_slope(pre_rows)).astype(jnp.bfloat16)
    pre_rows = grad_pre
    ffn_back = lax.psum_scatter(
        jnp.einsum("lrf,df->lrd", pre_rows, w_up, preferred_element_type=jnp.float32),
        "wide",
        scatter_dimension=0,
        tiled=True,
    )
    grad_first = grad_two + ffn_back
    grad_sum = norm_backward(grad_first, scaled_one, inv_one, norm1_gain)
    grad_attn = grad_sum.astype(jnp.bfloat16)
    grad_mix = project_back(grad_attn, w_out).astype(jnp.bfloat16)
    grad_heads = grad_mix.reshape(per_dev, row_count, H, E)
    pair_back = lax.all_gather(pair_own, "wide", axis=0, tiled=True)
    back_probs = attention_probs(
        query_heads, heads_of(pair_back, model_width, 0), own_seg, segments, prefix_vis, prefix_keys
    )
    seq_prob, pre_prob, seq_low, pre_low, row_max, prob_total = back_probs
    key_back = heads_of(pair_back, model_width, 0)
    value_back = heads_of(pair_back, model_width, 1)
    seq_grad = jnp.einsum(
        "crhe,lrhe->rhcl", grad_heads, value_back, preferred_element_type=jnp.float32
    )
    pre_grad = jnp.einsum(
        "crhe,phe->rhcp", grad_heads, prefix_vals, preferred_element_type=jnp.float32
    )
    grad_delta = (jnp.sum(seq_prob * seq_grad, axis=-1) + jnp.sum(pre_prob * pre_grad, axis=-1))[
        ..., None
    ]
    seq_ds = (seq_prob * (seq_grad - grad_delta)).astype(jnp.bfloat16)
    pre_ds = (pre_prob * (pre_grad - grad_delta)).astype(jnp.bfloat16)
    grad_query = jnp.einsum("rhcl,lrhe->crhe", seq_ds, key_back, preferred_element_type=jnp.float32)
    grad_query = grad_query + jnp.einsum(
        "rhcp,phe->crhe", pre_ds, prefix_keys, preferred_element_type=jnp.float32
    )
    grad_query = grad_query.reshape(per_dev, row_count, model_width).astype(jnp.bfloat16)
    prefix_kpart = jnp.einsum(
        "rhcp,crhe->phe", pre_ds, query_heads, preferred_element_type=jnp.float32
    ).reshape(P_SIZE, model_width)
    prefix_vpart = jnp.einsum(
        "rhcp,crhe->phe", pre_low, grad_heads, preferred_element_type=jnp.float32
    ).reshape(P_SIZE, model_width)
    key_part = jnp.einsum(
        "rhcl,crhe->lrhe", seq_ds, query_heads, preferred_element_type=jnp.float32
    )
    value_part = jnp.einsum(
        "rhcl,crhe->lrhe", seq_low, grad_heads, preferred_element_type=jnp.float32
    )
    seq_total = key_part.shape[0]
    key_grad, value_grad = (
        lax.psum_scatter(
            key_part.reshape(seq_total, row_count, model_width).astype(jnp.bfloat16),
            "wide",
            scatter_dimension=0,
            tiled=True,
        ).astype(jnp.float32),
        lax.psum_scatter(
            value_part.reshape(seq_total, row_count, model_width).astype(jnp.bfloat16),
            "wide",
            scatter_dimension=0,
            tiled=True,
        ).astype(jnp.float32),
    )
    input_grad = grad_sum + project_back(grad_query, w_query) * 0.125
    input_grad = (
        input_grad
        + project_back(key_grad.astype(jnp.bfloat16), w_key)
        + project_back(value_grad.astype(jnp.bfloat16), w_value)
    )
    prefix_key_grad, prefix_value_grad = lax.psum((prefix_kpart, prefix_vpart), ("rows", "wide"))
    return (block_out, input_grad, prefix_key_grad, prefix_value_grad)


def solution(mesh):
    in_specs = (
        P("wide", "rows", None),
        P("rows", None),
        P("rows", None),
        P(),
        P(),
        P(),
        P(),
        P(),
        P(),
        P(),
        P(),
        P(None, "wide"),
        P("wide", None),
        P(),
        P(),
        P("wide", "rows", None),
    )
    out_specs = (P("wide", "rows", None), P("wide", "rows", None), P(), P())
    return jax.shard_map(
        on_device, mesh=mesh, in_specs=in_specs, out_specs=out_specs, check_vma=False
    )
```

profile of v0, /device:TPU:0, one launch (start us, length us, event | category | flops | bytes accessed | tf_op | source)
XLA Modules:
  0.0 737.7 jit_solution(1522463249643954753)
XLA Ops:
  7.3 3.3 fusion.75
  13.5 3.9 multiply_convert_fusion.1
  26.1 48.4 %all-gather.4.cloned.1.call-done = bf16[1024,2,2048]{2,0,1:T(8,128)(2,1)} async-done(((bf16[256,2,2048]{2,0,1:T(8,128)(2,1)}), bf16[1024,2,2048]{2,0,1:T(8,128)(2,1)}) %all-gather.4.cloned.1.call-update) | async-done | bytes 8388624 | tf_op jit(solution)/shard_map/all_gather | solution.py:109
  74.5 5.9 fusion.148
  80.5 6.2 copy.120
  86.7 15.8 %select_reduce_fusion = (f32[2,16,256]{2,1,0:T(8,128)S(1)}, f32[2,16,256,1024]{3,2,1,0:T(8,128)}) fusion(pred[2,256,1024]{2,1,0:T(8,128)(4,1)} %broadcast_compare_fusion, bf16[256,2,16,64]{0,3,2,1:T(8,128)(2,1)S(1)} %bitcast.137, bf16[1024,2,16,64]{0,3,2,1:T(8,128)(2,1)} %bitcast.134), kind=kOutput, calls=%fused_computation.3 | convolution fusion | flops 1090510848 | bytes 39354368 | tf_op jit(solution)/shard_map/crhe,lrhe->rhcl/dot_general | solution.py:54
  102.5 14.7 %fusion.1 = f32[2,16,256]{2,1,0:T(8,128)S(1)} fusion(f32[2,16,256,1024]{3,2,1,0:T(8,128)} %get-tuple-element.35, f32[2,16,256]{2,1,0:T(8,128)S(1)} %copy_maximum_fusion, pred[2,256,1024]{2,1,0:T(8,128)(4,1)S(1)} %copy-done.14), kind=kLoop, calls=%fused_computation.5 | loop fusion | flops 25157632 | bytes 34144256 | tf_op jit(solution)/shard_map/reduce_sum | solution.py:67
  118.4 6.6 copy.117
  125.5 15.7 %fusion.42 = bf16[256,2,16,64]{0,3,2,1:T(8,128)(2,1)S(1)} fusion(f32[16,2,256,64]{2,3,0,1:T(8,128)S(1)} %fusion.96, bf16[1024,2,16,64]{0,3,2,1:T(8,128)(2,1)} %bitcast.141, f32[2,16,256,1024]{3,2,1,0:T(8,128)} %get-tuple-element.35, f32[2,16,256]{2,1,0:T(8,128)S(1)} %copy_add_fusion.1, f32[2,16,256]{2,1,0:T(8,128)S(1)} %copy_maximum_fusion, ...), kind=kOutput, calls=%fused_computation.62 | convolution fusion | flops 1108344832 | bytes 41484288 | tf_op jit(solution)/shard_map/rhcl,lrhe->crhe/dot_general | solution.py:115
  145.6 34.4 %all-gather.6.cloned.1.call-done = bf16[1024,2,1024]{2,0,1:T(8,128)(2,1)} async-done(((bf16[256,2,1024]{2,0,1:T(8,128)(2,1)}), bf16[1024,2,1024]{2,0,1:T(8,128)(2,1)}) %all-gather.6.cloned.1.call-update) | async-done | bytes 4194320 | tf_op jit(solution)/shard_map/all_gather | solution.py:134
  180.0 9.4 %fusion.57 = (u8[1024,1024]{1,0:T(8,128)(4,1)S(1)}, u8[1024,1024]{1,0:T(8,128)(4,1)S(1)}, f32[1024,2,1024]{2,0,1:T(8,128)S(1)}) fusion(bf16[1024,2,1024]{2,0,1:T(8,128)(2,1)} %all-gather.6.cloned.1.call-done, bf16[1024,1024]{1,0:T(8,128)(2,1)S(1)} %copy-done), kind=kOutput, calls=%fused_computation.92 | convolution fusion | flops 4320133120 | bytes 16777216 | tf_op jit(solution)/shard_map/lrd,df->lrf/dot_general | solution.py:132
  189.3 3.2 copy-done.56
  192.6 24.1 %fusion.21 = f32[1024,2,1024]{2,0,1:T(8,128)} fusion(f32[1024,2,1024]{2,0,1:T(8,128)S(1)} %get-tuple-element.40, bf16[1024,1024]{1,0:T(8,128)(2,1)S(1)} %copy-done.52, u8[1024,1024]{1,0:T(8,128)(4,1)S(1)} %get-tuple-element.21, u8[1024,1024]{1,0:T(8,128)(4,1)S(1)} %get-tuple-element.20), kind=kOutput, calls=%fused_computation.39 | convolution fusion | flops 4441767936 | bytes 20971520 | tf_op jit(solution)/shard_map/lrf,fd->lrd/dot_general | solution.py:137
  216.8 71.8 %reduce-scatter.5.cloned.1.call-done = f32[256,2,1024]{2,0,1:T(8,128)} async-done(((f32[1024,2,1024]{2,0,1:T(8,128)}), f32[256,2,1024]{2,0,1:T(8,128)}) %reduce-scatter.5.cloned.1.call-update) | async-done | bytes 2097168 | tf_op jit(solution)/shard_map/reduce_scatter | solution.py:136
  288.7 3.0 fusion.146
  295.2 34.6 %all-gather.8.cloned.1.call-done = bf16[1024,2,1024]{2,0,1:T(8,128)(2,1)} async-done(((bf16[256,2,1024]{2,0,1:T(8,128)(2,1)}), bf16[1024,2,1024]{2,0,1:T(8,128)(2,1)}) %all-gather.8.cloned.1.call-update) | async-done | bytes 4194320 | tf_op jit(solution)/shard_map/all_gather | solution.py:149
  329.7 14.6 %fusion.23 = f32[1024,2,1024]{2,0,1:T(8,128)} fusion(f32[1024,2,1024]{2,0,1:T(8,128)} %copy-done.56, bf16[1024,1024]{1,0:T(8,128)(2,1)S(1)} %copy-done, bf16[1024,2,1024]{2,0,1:T(8,128)(2,1)} %all-gather.8.cloned.1.call-done, bf16[1024,1024]{1,0:T(8,128)(2,1)} %param.28), kind=kOutput, calls=%fused_computation.40 | convolution fusion | flops 8610906112 | bytes 25165824 | tf_op jit(solution)/shard_map/lrf,df->lrd/dot_general | solution.py:157
  344.9 71.4 %reduce-scatter.7.cloned.1.call-done = f32[256,2,1024]{2,0,1:T(8,128)} async-done(((f32[1024,2,1024]{2,0,1:T(8,128)}), f32[256,2,1024]{2,0,1:T(8,128)}) %reduce-scatter.7.cloned.1.call-update) | async-done | bytes 2097168 | tf_op jit(solution)/shard_map/reduce_scatter | solution.py:156
  416.3 4.8 fusion.145
  427.3 26.7 %multiply_reduce_fusion = (f32[2,16,256]{2,1,0:T(8,128)S(1)}, f32[2,16,256,1024]{3,2,1,0:T(8,128)}) fusion(f32[2,16,256]{2,1,0:T(8,128)S(1)} %copy_add_fusion.1, f32[2,16,256]{2,1,0:T(8,128)S(1)} %copy_maximum_fusion, f32[2,16,256,1024]{3,2,1,0:T(8,128)} %get-tuple-element.35, pred[2,256,1024]{2,1,0:T(8,128)(4,1)S(1)} %copy-done.15, ...), kind=kOutput, calls=%fused_computation.1 | convolution fusion | flops 1115676672 | bytes 72974336 | tf_op jit(solution)/shard_map/crhe,lrhe->rhcl/dot_general | solution.py:174
  456.1 28.0 %multiply_convert_fusion = bf16[2,16,256,1024]{3,2,1,0:T(8,128)(2,1)} fusion(f32[2,16,256,1024]{3,2,1,0:T(8,128)} %get-tuple-element.42, f32[2,16,256]{2,1,0:T(8,128)S(1)} %copy_add_fusion, f32[2,16,256]{2,1,0:T(8,128)S(1)} %copy_add_fusion.1, f32[2,16,256]{2,1,0:T(8,128)S(1)} %copy_maximum_fusion, f32[2,16,256,1024]{3,2,1,0:T(8,128)} %get-tuple-element.35, ...), kind=kLoop, calls=%fused_computation | loop fusion | flops 50331648 | bytes 84508672 | tf_op jit(solution)/shard_map/convert_element_type | solution.py:183
  484.1 10.8 %convolution_convert_fusion = bf16[2,16,64,1024]{3,2,1,0:T(8,128)(2,1)} fusion(bf16[256,2,16,64]{0,3,2,1:T(8,128)(2,1)S(1)} %bitcast.138, bf16[2,16,256,1024]{3,2,1,0:T(8,128)(2,1)} %multiply_convert_fusion), kind=kOutput, calls=%fused_computation.41 | convolution fusion | flops 1075838976 | bytes 22020096 | tf_op jit(solution)/shard_map/rhcl,crhe->lrhe/dot_general | solution.py:196
  494.9 6.2 copy.139
  501.4 19.3 %fusion.25 = bf16[2,16,64,1024]{3,2,1,0:T(8,128)(2,1)} fusion(bf16[256,2,16,64]{0,3,2,1:T(8,128)(2,1)} %bitcast.145, f32[2,16,256,1024]{3,2,1,0:T(8,128)} %get-tuple-element.35, f32[2,16,256]{2,1,0:T(8,128)S(1)} %copy_add_fusion.1, f32[2,16,256]{2,1,0:T(8,128)S(1)} %copy_maximum_fusion, pred[2,256,1024]{2,1,0:T(8,128)(4,1)} %broadcast_compare_fusion), kind=kOutput, calls=%fused_computation.42 | convolution fusion | flops 1109393408 | bytes 39387136 | tf_op jit(solution)/shard_map/rhcl,crhe->lrhe/dot_general | solution.py:199
  520.7 6.2 copy.140
  538.1 13.8 %fusion.150 = f32[2,16,64,256]{3,2,1,0:T(8,128)} fusion(bf16[1024,2,16,64]{0,3,2,1:T(8,128)(2,1)} %bitcast.135, bf16[2,16,256,1024]{3,2,1,0:T(8,128)(2,1)} %multiply_convert_fusion), kind=kOutput, calls=%fused_computation.180 | convolution fusion | flops 1073741824 | bytes 23068672 | tf_op jit(solution)/shard_map/rhcl,lrhe->crhe/dot_general | solution.py:185
  554.0 4.7 fusion.52
  558.7 34.4 %reduce-scatter.11.cloned.1.call-done = bf16[256,2,1024]{2,0,1:T(8,128)(2,1)} async-done(((bf16[1024,2,1024]{2,0,1:T(8,128)(2,1)}), bf16[256,2,1024]{2,0,1:T(8,128)(2,1)}) %reduce-scatter.11.cloned.1.call-update) | async-done | bytes 1048592 | tf_op jit(solution)/shard_map/reduce_scatter | solution.py:210
  593.1 2.7 fusion.48
  596.3 3.9 add_add_fusion
  600.2 2.9 copy.146
  603.1 124.2 %all-reduce.3.cloned.1.call-done = (f32[64,1024]{1,0:T(8,128)}, f32[64,1024]{1,0:T(8,128)}) async-done(((f32[64,1024]{1,0:T(8,128)}, f32[64,1024]{1,0:T(8,128)}), (f32[64,1024]{1,0:T(8,128)}, f32[64,1024]{1,0:T(8,128)})) %all-reduce.3.cloned.1.call-update) | async-done | bytes 524304 | tf_op jit(solution)/shard_map/psum | solution.py:223
  (175 shorter events, 46.9 us)
Async XLA Ops:
  7.2 172.8 %copy-start = (bf16[1024,1024]{1,0:T(8,128)(2,1)S(1)}, bf16[1024,1024]{1,0:T(8,128)(2,1)}, u32[]{:S(2)}) copy-start(bf16[1024,1024]{1,0:T(8,128)(2,1)} %param.27) | copy-start | bytes 6291460
  7.2 67.3 %all-gather.4.cloned.1.call-start = ((), (), s32[]{:S(2)}) async-start(), calls=%async_computation.4 | async-start | bytes 10485760 | tf_op jit(solution)/shard_map/all_gather | solution.py:109
  13.4 166.6 %all-gather.6.cloned.1.call-start = ((), (), s32[]{:S(2)}) async-start(), calls=%async_computation.5 | async-start | bytes 5242880 | tf_op jit(solution)/shard_map/all_gather | solution.py:134
  19.0 67.7 %copy-start.8 = (bf16[256,2,1024]{0,2,1:T(8,128)(2,1)}, bf16[256,2,1024]{0,2,1:T(8,128)(2,1)S(1)}, u32[]{:S(2)}) copy-start(bf16[256,2,1024]{0,2,1:T(8,128)(2,1)S(1)} %copy.119) | copy-start | bytes 3145732
  19.2 61.3 %copy-start.20 = (bf16[64,16,64]{2,1,0:T(8,128)(2,1)}, bf16[64,16,64]{2,1,0:T(8,128)(2,1)S(1)}, u32[]{:S(2)}) copy-start(bf16[64,16,64]{2,1,0:T(8,128)(2,1)S(1)} %reshape.109) | copy-start | bytes 393220
  23.1 94.7 %copy-start.49 = (pred[2,64]{1,0:T(4,128)(4,1)}, pred[2,64]{1,0:T(4,128)(4,1)S(1)}, u32[]{:S(2)}) copy-start(pred[2,64]{1,0:T(4,128)(4,1)S(1)} %broadcast_compare_fusion.1) | copy-start | bytes 388
  86.7 15.8 %copy-start.14 = (pred[2,256,1024]{2,1,0:T(8,128)(4,1)S(1)}, pred[2,256,1024]{2,1,0:T(8,128)(4,1)}, u32[]{:S(2)}) copy-start(pred[2,256,1024]{2,1,0:T(8,128)(4,1)} %broadcast_compare_fusion) | copy-start | bytes 1572868
  142.6 278.5 %copy-start.37 = (f32[256,2]{0,1:T(2,128)}, f32[256,2]{0,1:T(2,128)S(1)}, u32[]{:S(2)}) copy-start(f32[256,2]{0,1:T(2,128)S(1)} %broadcast_multiply_fusion.5) | copy-start | bytes 6148
  143.9 277.2 %copy-start.39 = (f32[256,2]{0,1:T(2,128)}, f32[256,2]{0,1:T(2,128)S(1)}, u32[]{:S(2)}) copy-start(f32[256,2]{0,1:T(2,128)S(1)} %add_rsqrt_fusion.1) | copy-start | bytes 6148
  145.3 143.3 %reduce-scatter.5.cloned.1.call-start = ((), (), s32[]{:S(2)}) async-start(), calls=%async_computation.6 | async-start | bytes 10485760 | tf_op jit(solution)/shard_map/reduce_scatter | solution.py:136
  216.7 75.3 %copy-start.42 = (f32[1024]{0:T(1024)S(1)}, f32[1024]{0:T(1024)}, u32[]{:S(2)}) copy-start(f32[1024]{0:T(1024)} %param.29) | copy-start | bytes 12292
  216.8 113.0 %all-gather.8.cloned.1.call-start = ((), (), s32[]{:S(2)}) async-start(), calls=%async_computation.7 | async-start | bytes 5242880 | tf_op jit(solution)/shard_map/all_gather | solution.py:149
  295.1 121.2 %reduce-scatter.7.cloned.1.call-start = ((), (), s32[]{:S(2)}) async-start(), calls=%async_computation.8 | async-start | bytes 10485760 | tf_op jit(solution)/shard_map/reduce_scatter | solution.py:156
  344.4 71.9 %copy-start.3 = (f32[256,2,1024]{2,0,1:T(8,128)S(1)}, f32[256,2,1024]{2,0,1:T(8,128)}, u32[]{:S(2)}) copy-start(f32[256,2,1024]{2,0,1:T(8,128)} %copy-done.2) | copy-start | bytes 6291460
  344.4 71.9 %copy-start.51 = (f32[1024]{0:T(1024)S(1)}, f32[1024]{0:T(1024)}, u32[]{:S(2)}) copy-start(f32[1024]{0:T(1024)} %param.30) | copy-start | bytes 12292
  344.4 209.6 %reduce-scatter.9.cloned.1.call-start = ((), (), s32[]{:S(2)}) async-start(), calls=%async_computation.9 | async-start | bytes 5242880 | tf_op jit(solution)/shard_map/reduce_scatter | solution.py:204
  427.2 26.8 %copy-start.7 = (f32[16,256,2,64]{1,3,2,0:T(8,128)S(1)}, f32[16,256,2,64]{1,3,2,0:T(8,128)}, u32[]{:S(2)}) copy-start(f32[16,256,2,64]{1,3,2,0:T(8,128)} %get-tuple-element.37) | copy-start | bytes 6291460
  427.2 26.8 %copy-start.19 = (bf16[256,2,1024]{0,2,1:T(8,128)(2,1)S(1)}, bf16[256,2,1024]{0,2,1:T(8,128)(2,1)}, u32[]{:S(2)}) copy-start(bf16[256,2,1024]{0,2,1:T(8,128)(2,1)} %copy.131) | copy-start | bytes 3145732
  427.3 26.8 %copy-start.26 = (bf16[64,16,64]{2,1,0:T(8,128)(2,1)S(1)}, bf16[64,16,64]{2,1,0:T(8,128)(2,1)}, u32[]{:S(2)}) copy-start(bf16[64,16,64]{2,1,0:T(8,128)(2,1)} %reshape.110) | copy-start | bytes 393220
  427.3 26.8 %copy-start.31 = (f32[2,16,256]{2,0,1:T(2,128)S(1)}, f32[2,16,256]{2,0,1:T(2,128)}, u32[]{:S(2)}) copy-start(f32[2,16,256]{2,0,1:T(2,128)} %copy-done.30) | copy-start | bytes 98308
  427.3 26.8 %copy-start.33 = (f32[2,16,256]{2,0,1:T(2,128)S(1)}, f32[2,16,256]{2,0,1:T(2,128)}, u32[]{:S(2)}) copy-start(f32[2,16,256]{2,0,1:T(2,128)} %copy-done.32) | copy-start | bytes 98308
  427.3 26.8 %copy-start.50 = (pred[2,64]{1,0:T(4,128)(4,1)S(1)}, pred[2,64]{1,0:T(4,128)(4,1)}, u32[]{:S(2)}) copy-start(pred[2,64]{1,0:T(4,128)(4,1)} %copy-done.49) | copy-start | bytes 388
  456.1 28.1 %copy-start.34 = (f32[2,16,256]{2,1,0:T(8,128)}, f32[2,16,256]{2,1,0:T(8,128)S(1)}, u32[]{:S(2)}) copy-start(f32[2,16,256]{2,1,0:T(8,128)S(1)} %copy_add_fusion) | copy-start | bytes 98308
  456.1 28.1 %copy-start.9 = (bf16[256,2,1024]{0,2,1:T(8,128)(2,1)S(1)}, bf16[256,2,1024]{0,2,1:T(8,128)(2,1)}, u32[]{:S(2)}) copy-start(bf16[256,2,1024]{0,2,1:T(8,128)(2,1)} %copy-done.8) | copy-start | bytes 3145732
  501.2 91.9 %reduce-scatter.11.cloned.1.call-start = ((), (), s32[]{:S(2)}) async-start(), calls=%async_computation.10 | async-start | bytes 5242880 | tf_op jit(solution)/shard_map/reduce_scatter | solution.py:210
  527.0 200.3 %all-reduce.3.cloned.1.call-start = ((), (), s32[]{:S(2)}) async-start(), calls=%async_computation.11 | async-start | bytes 1048576 | tf_op jit(solution)/shard_map/psum | solution.py:223
  553.9 39.2 %copy-start.54 = (bf16[1024,1024]{1,0:T(8,128)(2,1)S(1)}, bf16[1024,1024]{1,0:T(8,128)(2,1)}, u32[]{:S(2)}) copy-start(bf16[1024,1024]{1,0:T(8,128)(2,1)} %param.23) | copy-start | bytes 6291460
  558.7 37.1 %copy-start.38 = (f32[256,2]{0,1:T(2,128)S(1)}, f32[256,2]{0,1:T(2,128)}, u32[]{:S(2)}) copy-start(f32[256,2]{0,1:T(2,128)} %copy-done.37) | copy-start | bytes 6148
  558.7 37.1 %copy-start.40 = (f32[256,2]{0,1:T(2,128)S(1)}, f32[256,2]{0,1:T(2,128)}, u32[]{:S(2)}) copy-start(f32[256,2]{0,1:T(2,128)} %copy-done.39) | copy-start | bytes 6148
  558.7 37.1 %copy-start.44 = (f32[256,2]{0,1:T(2,128)S(1)}, f32[256,2]{0,1:T(2,128)}, u32[]{:S(2)}) copy-start(f32[256,2]{0,1:T(2,128)} %copy-done.43) | copy-start | bytes 6148
  558.7 37.1 %copy-start.46 = (f32[256,2]{0,1:T(2,128)S(1)}, f32[256,2]{0,1:T(2,128)}, u32[]{:S(2)}) copy-start(f32[256,2]{0,1:T(2,128)} %copy-done.45) | copy-start | bytes 6148
  596.3 134.4 %copy-start.1 = (bf16[1024,1024]{1,0:T(8,128)(2,1)S(1)}, bf16[1024,1024]{1,0:T(8,128)(2,1)}, u32[]{:S(2)}) copy-start(bf16[1024,1024]{1,0:T(8,128)(2,1)} %param.27) | copy-start | bytes 6291460
  (33 other events, 199.3 us)
Sparse Core Ops, SparseCore 0:
  13.5 60.9 all-gather.3
  145.4 34.4 all-gather.5
  216.9 71.7 reduce-scatter.4
  295.2 34.4 all-gather.7
  344.5 71.7 reduce-scatter.6
  501.3 44.5 reduce-scatter.8
  548.6 44.5 reduce-scatter.10
  599.2 128.1 all-reduce.2
where the time goes:
time: 742 us; the launch traced here: 738 us
  waiting for transfers between devices  419 us (56%)
  matrix products  182 us (25%)
  other arithmetic  61.8 us (8%)
  local copies, waits for them, and re-layouts  58 us (8%)
  between operations  15 us (2%)
    psum x1, waiting for transfers between devices, on_device(): lax.psum((prefix_kpart, prefix_vpart), ('rows', 'wide'))  124 us
    reduce_scatter x1, waiting for transfers between devices, on_device(): lax.psum_scatter(jnp.einsum('lrf,fd->lrd', hidden_act, w_down, preferred_...  71.8 us
    reduce_scatter x1, waiting for transfers between devices, on_device(): lax.psum_scatter(jnp.einsum('lrf,df->lrd', pre_rows, w_up, preferred_elem...  71.4 us
    all_gather x1, waiting for transfers between devices, on_device(): pair_all = lax.all_gather(pair_own, 'wide', axis=0, tiled=True)  48.4 us
    all_gather x1, waiting for transfers between devices, on_device(): lax.all_gather(grad_ffn, 'wide', axis=0, tiled=True)  34.6 us
    reduce_scatter x1, waiting for transfers between devices, on_device(): lax.psum_scatter(value_part.reshape(seq_total, row_count, model_width).as...  34.4 us
    all_gather x1, waiting for transfers between devices, on_device(): hidden_pre = up_rows(lax.all_gather(normed_low, 'wide', axis=0, tiled=True))  34.4 us
    convert_element_type x1, other arithmetic, on_device(): seq_ds = (seq_prob * (seq_grad - grad_delta)).astype(jnp.bfloat16)  28 us
  transfers between devices with their start and end apart: 8, of which 7 were waited for; matrix products, arithmetic and copies ran while one was open for 11% of the time, Pallas kernels for 0%

commit v1 on v0

--- a/solution.py
+++ b/solution.py
@@ -10,6 +10,11 @@
 neg_large = -1e30
 root_half = 0.7071067811865476
 inv_root_tau = 0.3989422804014327
+
+
+def by_each_axis(x, inner_axis, outer_axis):
+    inner = lax.psum(x, inner_axis)
+    return lax.psum(inner, outer_axis)
 
 
 def norm_forward(summed, norm_gain, norm_bias):
@@ -220,7 +225,7 @@
         + project_back(key_grad.astype(jnp.bfloat16), w_key)
         + project_back(value_grad.astype(jnp.bfloat16), w_value)
     )
-    prefix_key_grad, prefix_value_grad = lax.psum((prefix_kpart, prefix_vpart), ("rows", "wide"))
+    prefix_key_grad, prefix_value_grad = by_each_axis((prefix_kpart, prefix_vpart), "wide", "rows")
     return (block_out, input_grad, prefix_key_grad, prefix_value_grad)
 
 

time: 742 us -> 707 us (0.953)
  waiting for transfers between devices: 419 us -> 389 us
    psum x1 -> x2, waiting for transfers between devices: 124 us -> 66.2 us  [the longest x1 66.1 us: by_each_axis(): return lax.psum(inner, outer_axis)]
    reduce_scatter x1, waiting for transfers between devices: 0.02 us -> 19.8 us  [on_device(): lax.psum_scatter(key_part.reshape(seq_total, row_count, model_width).asty...]
    reduce_scatter x1, waiting for transfers between devices: 34.4 us -> 42.7 us  [on_device(): lax.psum_scatter(value_part.reshape(seq_total, row_count, model_width).as...]
  transfers between devices with their start and end apart: 8 -> 9, of which waited for: 7 -> 8; matrix products, arithmetic and copies ran while one was open for 11% -> 12% of each run, Pallas kernels for 0% -> 0%
where the time goes in v1:
time: 707 us; the launch traced here: 703 us
  waiting for transfers between devices  389 us (55%)
  matrix products  177 us (25%)
  local copies, waits for them, and re-layouts  60.2 us (9%)
  other arithmetic  59.9 us (8%)
  between operations  14.7 us (2%)
    reduce_scatter x1, waiting for transfers between devices, on_device(): lax.psum_scatter(jnp.einsum('lrf,fd->lrd', hidden_act, w_down, preferred_...  71.8 us
    reduce_scatter x1, waiting for transfers between devices, on_device(): lax.psum_scatter(jnp.einsum('lrf,df->lrd', pre_rows, w_up, preferred_elem...  71.6 us
    psum x1, waiting for transfers between devices, by_each_axis(): return lax.psum(inner, outer_axis)  66.1 us
    all_gather x1, waiting for transfers between devices, on_device(): pair_all = lax.all_gather(pair_own, 'wide', axis=0, tiled=True)  48.4 us
    reduce_scatter x1, waiting for transfers between devices, on_device(): lax.psum_scatter(value_part.reshape(seq_total, row_count, model_width).as...  42.7 us
    all_gather x1, waiting for transfers between devices, on_device(): lax.all_gather(grad_ffn, 'wide', axis=0, tiled=True)  34.6 us
    all_gather x1, waiting for transfers between devices, on_device(): hidden_pre = up_rows(lax.all_gather(normed_low, 'wide', axis=0, tiled=True))  34.2 us
    convert_element_type x1, other arithmetic, on_device(): seq_ds = (seq_prob * (seq_grad - grad_delta)).astype(jnp.bfloat16)  27.8 us
  transfers between devices with their start and end apart: 9, of which 8 were waited for; matrix products, arithmetic and copies ran while one was open for 12% of the time, Pallas kernels for 0%

profile of v1, /device:TPU:0, one launch (start us, length us, event | category | flops | bytes accessed | tf_op | source)
XLA Modules:
  0.0 702.9 jit_solution(12681732265456038789)
XLA Ops:
  7.3 3.3 fusion.75
  13.5 3.9 multiply_convert_fusion.1
  26.1 48.4 %all-gather.4.cloned.1.call-done = bf16[1024,2,2048]{2,0,1:T(8,128)(2,1)} async-done(((bf16[256,2,2048]{2,0,1:T(8,128)(2,1)}), bf16[1024,2,2048]{2,0,1:T(8,128)(2,1)}) %all-gather.4.cloned.1.call-update) | async-done | bytes 8388624 | tf_op jit(solution)/shard_map/all_gather | solution.py:114
  74.5 6.0 fusion.148
  80.5 6.2 copy.120
  86.7 15.8 %select_reduce_fusion = (f32[2,16,256]{2,1,0:T(8,128)S(1)}, f32[2,16,256,1024]{3,2,1,0:T(8,128)}) fusion(pred[2,256,1024]{2,1,0:T(8,128)(4,1)} %broadcast_compare_fusion, bf16[256,2,16,64]{0,3,2,1:T(8,128)(2,1)S(1)} %bitcast.137, bf16[1024,2,16,64]{0,3,2,1:T(8,128)(2,1)} %bitcast.134), kind=kOutput, calls=%fused_computation.3 | convolution fusion | flops 1090510848 | bytes 39354368 | tf_op jit(solution)/shard_map/crhe,lrhe->rhcl/dot_general | solution.py:59
  102.6 14.7 %fusion.1 = f32[2,16,256]{2,1,0:T(8,128)S(1)} fusion(f32[2,16,256,1024]{3,2,1,0:T(8,128)} %get-tuple-element.37, f32[2,16,256]{2,1,0:T(8,128)S(1)} %copy_maximum_fusion, pred[2,256,1024]{2,1,0:T(8,128)(4,1)S(1)} %copy-done.15), kind=kLoop, calls=%fused_computation.5 | loop fusion | flops 25157632 | bytes 34144256 | tf_op jit(solution)/shard_map/reduce_sum | solution.py:72
  118.5 6.6 copy.117
  125.5 15.7 %fusion.42 = bf16[256,2,16,64]{0,3,2,1:T(8,128)(2,1)S(1)} fusion(f32[16,2,256,64]{2,3,0,1:T(8,128)S(1)} %fusion.96, bf16[1024,2,16,64]{0,3,2,1:T(8,128)(2,1)} %bitcast.141, f32[2,16,256,1024]{3,2,1,0:T(8,128)} %get-tuple-element.37, f32[2,16,256]{2,1,0:T(8,128)S(1)} %copy_add_fusion.1, f32[2,16,256]{2,1,0:T(8,128)S(1)} %copy_maximum_fusion, ...), kind=kOutput, calls=%fused_computation.62 | convolution fusion | flops 1108344832 | bytes 41484288 | tf_op jit(solution)/shard_map/rhcl,lrhe->crhe/dot_general | solution.py:120
  145.8 34.2 %all-gather.6.cloned.1.call-done = bf16[1024,2,1024]{2,0,1:T(8,128)(2,1)} async-done(((bf16[256,2,1024]{2,0,1:T(8,128)(2,1)}), bf16[1024,2,1024]{2,0,1:T(8,128)(2,1)}) %all-gather.6.cloned.1.call-update) | async-done | bytes 4194320 | tf_op jit(solution)/shard_map/all_gather | solution.py:139
  180.0 9.4 %fusion.57 = (u8[1024,1024]{1,0:T(8,128)(4,1)S(1)}, u8[1024,1024]{1,0:T(8,128)(4,1)S(1)}, f32[1024,2,1024]{2,0,1:T(8,128)S(1)}) fusion(bf16[1024,2,1024]{2,0,1:T(8,128)(2,1)} %all-gather.6.cloned.1.call-done, bf16[1024,1024]{1,0:T(8,128)(2,1)S(1)} %copy-done), kind=kOutput, calls=%fused_computation.92 | convolution fusion | flops 4320133120 | bytes 16777216 | tf_op jit(solution)/shard_map/lrd,df->lrf/dot_general | solution.py:137
  189.4 3.2 copy-done.56
  192.6 24.2 %fusion.21 = f32[1024,2,1024]{2,0,1:T(8,128)} fusion(f32[1024,2,1024]{2,0,1:T(8,128)S(1)} %get-tuple-element.42, bf16[1024,1024]{1,0:T(8,128)(2,1)S(1)} %copy-done.52, u8[1024,1024]{1,0:T(8,128)(4,1)S(1)} %get-tuple-element.21, u8[1024,1024]{1,0:T(8,128)(4,1)S(1)} %get-tuple-element.20), kind=kOutput, calls=%fused_computation.39 | convolution fusion | flops 4441767936 | bytes 20971520 | tf_op jit(solution)/shard_map/lrf,fd->lrd/dot_general | solution.py:142
  216.9 71.8 %reduce-scatter.5.cloned.1.call-done = f32[256,2,1024]{2,0,1:T(8,128)} async-done(((f32[1024,2,1024]{2,0,1:T(8,128)}), f32[256,2,1024]{2,0,1:T(8,128)}) %reduce-scatter.5.cloned.1.call-update) | async-done | bytes 2097168 | tf_op jit(solution)/shard_map/reduce_scatter | solution.py:141
  288.7 3.0 fusion.146
  295.2 34.6 %all-gather.8.cloned.1.call-done = bf16[1024,2,1024]{2,0,1:T(8,128)(2,1)} async-done(((bf16[256,2,1024]{2,0,1:T(8,128)(2,1)}), bf16[1024,2,1024]{2,0,1:T(8,128)(2,1)}) %all-gather.8.cloned.1.call-update) | async-done | bytes 4194320 | tf_op jit(solution)/shard_map/all_gather | solution.py:154
  329.8 14.7 %fusion.23 = f32[1024,2,1024]{2,0,1:T(8,128)} fusion(f32[1024,2,1024]{2,0,1:T(8,128)} %copy-done.56, bf16[1024,1024]{1,0:T(8,128)(2,1)S(1)} %copy-done, bf16[1024,2,1024]{2,0,1:T(8,128)(2,1)} %all-gather.8.cloned.1.call-done, bf16[1024,1024]{1,0:T(8,128)(2,1)} %param.28), kind=kOutput, calls=%fused_computation.40 | convolution fusion | flops 8610906112 | bytes 25165824 | tf_op jit(solution)/shard_map/lrf,df->lrd/dot_general | solution.py:162
  344.7 71.6 %reduce-scatter.7.cloned.1.call-done = f32[256,2,1024]{2,0,1:T(8,128)} async-done(((f32[1024,2,1024]{2,0,1:T(8,128)}), f32[256,2,1024]{2,0,1:T(8,128)}) %reduce-scatter.7.cloned.1.call-update) | async-done | bytes 2097168 | tf_op jit(solution)/shard_map/reduce_scatter | solution.py:161
  416.4 4.8 fusion.145
  427.4 26.7 %multiply_reduce_fusion = (f32[2,16,256]{2,1,0:T(8,128)S(1)}, f32[2,16,256,1024]{3,2,1,0:T(8,128)}) fusion(f32[2,16,256]{2,1,0:T(8,128)S(1)} %copy_add_fusion.1, f32[2,16,256]{2,1,0:T(8,128)S(1)} %copy_maximum_fusion, f32[2,16,256,1024]{3,2,1,0:T(8,128)} %get-tuple-element.37, pred[2,256,1024]{2,1,0:T(8,128)(4,1)S(1)} %copy-done.16, ...), kind=kOutput, calls=%fused_computation.1 | convolution fusion | flops 1115676672 | bytes 72974336 | tf_op jit(solution)/shard_map/crhe,lrhe->rhcl/dot_general | solution.py:179
  461.3 27.8 %multiply_convert_fusion = bf16[2,16,256,1024]{3,2,1,0:T(8,128)(2,1)} fusion(f32[2,16,256,1024]{3,2,1,0:T(8,128)} %get-tuple-element.44, f32[2,16,256]{2,1,0:T(8,128)S(1)} %copy_add_fusion, f32[2,16,256]{2,1,0:T(8,128)S(1)} %copy_add_fusion.1, f32[2,16,256]{2,1,0:T(8,128)S(1)} %copy_maximum_fusion, f32[2,16,256,1024]{3,2,1,0:T(8,128)} %get-tuple-element.37, ...), kind=kLoop, calls=%fused_computation | loop fusion | flops 50331648 | bytes 84508672 | tf_op jit(solution)/shard_map/convert_element_type | solution.py:188
  489.1 10.9 %convolution_convert_fusion = bf16[2,16,64,1024]{3,2,1,0:T(8,128)(2,1)} fusion(bf16[256,2,16,64]{0,3,2,1:T(8,128)(2,1)S(1)} %bitcast.139, bf16[2,16,256,1024]{3,2,1,0:T(8,128)(2,1)} %multiply_convert_fusion), kind=kOutput, calls=%fused_computation.41 | convolution fusion | flops 1075838976 | bytes 22020096 | tf_op jit(solution)/shard_map/rhcl,crhe->lrhe/dot_general | solution.py:201
  500.0 6.3 copy.139
  507.4 15.8 %fusion.25 = bf16[2,16,64,1024]{3,2,1,0:T(8,128)(2,1)} fusion(bf16[256,2,16,64]{0,3,2,1:T(8,128)(2,1)S(1)} %bitcast.147, f32[2,16,256,1024]{3,2,1,0:T(8,128)} %get-tuple-element.37, f32[2,16,256]{2,1,0:T(8,128)S(1)} %copy_add_fusion.1, f32[2,16,256]{2,1,0:T(8,128)S(1)} %copy_maximum_fusion, pred[2,256,1024]{2,1,0:T(8,128)(4,1)S(1)} %copy-done.17), kind=kOutput, calls=%fused_computation.42 | convolution fusion | flops 1109393408 | bytes 39387136 | tf_op jit(solution)/shard_map/rhcl,crhe->lrhe/dot_general | solution.py:204
  523.2 6.2 copy.140
  533.2 14.4 %fusion.150 = f32[2,16,64,256]{3,2,1,0:T(8,128)} fusion(bf16[1024,2,16,64]{0,3,2,1:T(8,128)(2,1)} %bitcast.135, bf16[2,16,256,1024]{3,2,1,0:T(8,128)(2,1)} %multiply_convert_fusion), kind=kOutput, calls=%fused_computation.180 | convolution fusion | flops 1073741824 | bytes 23068672 | tf_op jit(solution)/shard_map/rhcl,lrhe->crhe/dot_general | solution.py:190
  549.6 19.8 %reduce-scatter.9.cloned.1.call-done = bf16[256,2,1024]{2,0,1:T(8,128)(2,1)} async-done(((bf16[1024,2,1024]{2,0,1:T(8,128)(2,1)}), bf16[256,2,1024]{2,0,1:T(8,128)(2,1)}) %reduce-scatter.9.cloned.1.call-update) | async-done | bytes 1048592 | tf_op jit(solution)/shard_map/reduce_scatter | solution.py:209
  569.5 4.6 fusion.52
  574.0 42.7 %reduce-scatter.11.cloned.1.call-done = bf16[256,2,1024]{2,0,1:T(8,128)(2,1)} async-done(((bf16[1024,2,1024]{2,0,1:T(8,128)(2,1)}), bf16[256,2,1024]{2,0,1:T(8,128)(2,1)}) %reduce-scatter.11.cloned.1.call-update) | async-done | bytes 1048592 | tf_op jit(solution)/shard_map/reduce_scatter | solution.py:215
  619.9 3.9 add_add_fusion
  623.8 2.9 copy.146
  626.7 66.1 %all-reduce.5.cloned.1.call-done = (f32[64,1024]{1,0:T(8,128)}, f32[64,1024]{1,0:T(8,128)}) async-done(((f32[64,1024]{1,0:T(8,128)}, f32[64,1024]{1,0:T(8,128)}), (f32[64,1024]{1,0:T(8,128)}, f32[64,1024]{1,0:T(8,128)})) %all-reduce.5.cloned.1.call-update) | async-done | bytes 524304 | tf_op jit(solution)/shard_map/psum | solution.py:17
  (178 shorter events, 48.2 us)
Async XLA Ops:
  7.2 172.8 %copy-start = (bf16[1024,1024]{1,0:T(8,128)(2,1)S(1)}, bf16[1024,1024]{1,0:T(8,128)(2,1)}, u32[]{:S(2)}) copy-start(bf16[1024,1024]{1,0:T(8,128)(2,1)} %param.27) | copy-start | bytes 6291460
  7.2 67.3 %all-gather.4.cloned.1.call-start = ((), (), s32[]{:S(2)}) async-start(), calls=%async_computation.4 | async-start | bytes 10485760 | tf_op jit(solution)/shard_map/all_gather | solution.py:114
  13.4 166.6 %all-gather.6.cloned.1.call-start = ((), (), s32[]{:S(2)}) async-start(), calls=%async_computation.5 | async-start | bytes 5242880 | tf_op jit(solution)/shard_map/all_gather | solution.py:139
  19.0 67.7 %copy-start.8 = (bf16[256,2,1024]{0,2,1:T(8,128)(2,1)}, bf16[256,2,1024]{0,2,1:T(8,128)(2,1)S(1)}, u32[]{:S(2)}) copy-start(bf16[256,2,1024]{0,2,1:T(8,128)(2,1)S(1)} %copy.119) | copy-start | bytes 3145732
  19.2 61.3 %copy-start.23 = (bf16[64,16,64]{2,1,0:T(8,128)(2,1)}, bf16[64,16,64]{2,1,0:T(8,128)(2,1)S(1)}, u32[]{:S(2)}) copy-start(bf16[64,16,64]{2,1,0:T(8,128)(2,1)S(1)} %reshape.109) | copy-start | bytes 393220
  23.1 94.7 %copy-start.49 = (pred[2,64]{1,0:T(4,128)(4,1)}, pred[2,64]{1,0:T(4,128)(4,1)S(1)}, u32[]{:S(2)}) copy-start(pred[2,64]{1,0:T(4,128)(4,1)S(1)} %broadcast_compare_fusion.1) | copy-start | bytes 388
  86.7 15.9 %copy-start.15 = (pred[2,256,1024]{2,1,0:T(8,128)(4,1)S(1)}, pred[2,256,1024]{2,1,0:T(8,128)(4,1)}, u32[]{:S(2)}) copy-start(pred[2,256,1024]{2,1,0:T(8,128)(4,1)} %broadcast_compare_fusion) | copy-start | bytes 1572868
  142.7 278.6 %copy-start.37 = (f32[256,2]{0,1:T(2,128)}, f32[256,2]{0,1:T(2,128)S(1)}, u32[]{:S(2)}) copy-start(f32[256,2]{0,1:T(2,128)S(1)} %broadcast_multiply_fusion.5) | copy-start | bytes 6148
  144.0 277.3 %copy-start.39 = (f32[256,2]{0,1:T(2,128)}, f32[256,2]{0,1:T(2,128)S(1)}, u32[]{:S(2)}) copy-start(f32[256,2]{0,1:T(2,128)S(1)} %add_rsqrt_fusion.1) | copy-start | bytes 6148
  145.4 143.4 %reduce-scatter.5.cloned.1.call-start = ((), (), s32[]{:S(2)}) async-start(), calls=%async_computation.6 | async-start | bytes 10485760 | tf_op jit(solution)/shard_map/reduce_scatter | solution.py:141
  216.8 75.2 %copy-start.42 = (f32[1024]{0:T(1024)S(1)}, f32[1024]{0:T(1024)}, u32[]{:S(2)}) copy-start(f32[1024]{0:T(1024)} %param.29) | copy-start | bytes 12292
  216.9 112.9 %all-gather.8.cloned.1.call-start = ((), (), s32[]{:S(2)}) async-start(), calls=%async_computation.7 | async-start | bytes 5242880 | tf_op jit(solution)/shard_map/all_gather | solution.py:154
  295.2 121.2 %reduce-scatter.7.cloned.1.call-start = ((), (), s32[]{:S(2)}) async-start(), calls=%async_computation.8 | async-start | bytes 10485760 | tf_op jit(solution)/shard_map/reduce_scatter | solution.py:161
  344.5 71.9 %copy-start.3 = (f32[256,2,1024]{2,0,1:T(8,128)S(1)}, f32[256,2,1024]{2,0,1:T(8,128)}, u32[]{:S(2)}) copy-start(f32[256,2,1024]{2,0,1:T(8,128)} %copy-done.2) | copy-start | bytes 6291460
  344.5 71.9 %copy-start.51 = (f32[1024]{0:T(1024)S(1)}, f32[1024]{0:T(1024)}, u32[]{:S(2)}) copy-start(f32[1024]{0:T(1024)} %param.30) | copy-start | bytes 12292
  344.5 205.1 %all-reduce.7.cloned.1.call-start = ((), (), s32[]{:S(2)}) async-start(), calls=%async_computation.12 | async-start | bytes 1048576 | tf_op jit(solution)/shard_map/psum | solution.py:16
  427.4 26.8 %copy-start.12 = (bf16[2,16,256,64]{2,3,0,1:T(8,128)(2,1)S(1)}, bf16[2,16,256,64]{2,3,0,1:T(8,128)(2,1)}, u32[]{:S(2)}) copy-start(bf16[2,16,256,64]{2,3,0,1:T(8,128)(2,1)} %copy-done.11) | copy-start | bytes 3145732
  427.4 26.8 %copy-start.21 = (bf16[256,2,1024]{0,2,1:T(8,128)(2,1)S(1)}, bf16[256,2,1024]{0,2,1:T(8,128)(2,1)}, u32[]{:S(2)}) copy-start(bf16[256,2,1024]{0,2,1:T(8,128)(2,1)} %copy.131) | copy-start | bytes 3145732
  427.4 28.0 %copy-start.7 = (f32[16,256,2,64]{1,3,2,0:T(8,128)S(1)}, f32[16,256,2,64]{1,3,2,0:T(8,128)}, u32[]{:S(2)}) copy-start(f32[16,256,2,64]{1,3,2,0:T(8,128)} %get-tuple-element.39) | copy-start | bytes 6291460
  427.4 28.0 %copy-start.28 = (bf16[64,16,64]{2,1,0:T(8,128)(2,1)S(1)}, bf16[64,16,64]{2,1,0:T(8,128)(2,1)}, u32[]{:S(2)}) copy-start(bf16[64,16,64]{2,1,0:T(8,128)(2,1)} %reshape.110) | copy-start | bytes 393220
  427.4 28.0 %copy-start.33 = (f32[2,16,256]{2,0,1:T(2,128)S(1)}, f32[2,16,256]{2,0,1:T(2,128)}, u32[]{:S(2)}) copy-start(f32[2,16,256]{2,0,1:T(2,128)} %copy-done.32) | copy-start | bytes 98308
  427.4 28.0 %copy-start.35 = (f32[2,16,256]{2,0,1:T(2,128)S(1)}, f32[2,16,256]{2,0,1:T(2,128)}, u32[]{:S(2)}) copy-start(f32[2,16,256]{2,0,1:T(2,128)} %copy-done.34) | copy-start | bytes 98308
  427.4 28.0 %copy-start.50 = (pred[2,64]{1,0:T(4,128)(4,1)S(1)}, pred[2,64]{1,0:T(4,128)(4,1)}, u32[]{:S(2)}) copy-start(pred[2,64]{1,0:T(4,128)(4,1)} %copy-done.49) | copy-start | bytes 388
  489.0 80.4 %reduce-scatter.9.cloned.1.call-start = ((), (), s32[]{:S(2)}) async-start(), calls=%async_computation.9 | async-start | bytes 5242880 | tf_op jit(solution)/shard_map/reduce_scatter | solution.py:209
  506.2 110.5 %reduce-scatter.11.cloned.1.call-start = ((), (), s32[]{:S(2)}) async-start(), calls=%async_computation.10 | async-start | bytes 5242880 | tf_op jit(solution)/shard_map/reduce_scatter | solution.py:215
  529.5 163.3 %all-reduce.5.cloned.1.call-start = ((), (), s32[]{:S(2)}) async-start(), calls=%async_computation.11 | async-start | bytes 1048576 | tf_op jit(solution)/shard_map/psum | solution.py:17
  549.6 67.1 %copy-start.54 = (bf16[1024,1024]{1,0:T(8,128)(2,1)S(1)}, bf16[1024,1024]{1,0:T(8,128)(2,1)}, u32[]{:S(2)}) copy-start(bf16[1024,1024]{1,0:T(8,128)(2,1)} %param.23) | copy-start | bytes 6291460
  574.0 45.4 %copy-start.38 = (f32[256,2]{0,1:T(2,128)S(1)}, f32[256,2]{0,1:T(2,128)}, u32[]{:S(2)}) copy-start(f32[256,2]{0,1:T(2,128)} %copy-done.37) | copy-start | bytes 6148
  574.0 45.4 %copy-start.40 = (f32[256,2]{0,1:T(2,128)S(1)}, f32[256,2]{0,1:T(2,128)}, u32[]{:S(2)}) copy-start(f32[256,2]{0,1:T(2,128)} %copy-done.39) | copy-start | bytes 6148
  574.0 45.4 %copy-start.44 = (f32[256,2]{0,1:T(2,128)S(1)}, f32[256,2]{0,1:T(2,128)}, u32[]{:S(2)}) copy-start(f32[256,2]{0,1:T(2,128)} %copy-done.43) | copy-start | bytes 6148
  574.0 45.4 %copy-start.46 = (f32[256,2]{0,1:T(2,128)S(1)}, f32[256,2]{0,1:T(2,128)}, u32[]{:S(2)}) copy-start(f32[256,2]{0,1:T(2,128)} %copy-done.45) | copy-start | bytes 6148
  619.9 76.3 %copy-start.1 = (bf16[1024,1024]{1,0:T(8,128)(2,1)S(1)}, bf16[1024,1024]{1,0:T(8,128)(2,1)}, u32[]{:S(2)}) copy-start(bf16[1024,1024]{1,0:T(8,128)(2,1)} %param.27) | copy-start | bytes 6291460
  (34 other events, 187.6 us)
Sparse Core Ops, SparseCore 0:
  13.5 60.9 all-gather.3
  145.5 34.4 all-gather.5
  217.0 71.7 reduce-scatter.4
  295.3 34.4 all-gather.7
  344.6 71.6 reduce-scatter.6
  489.2 33.1 all-reduce.6
  524.9 44.5 reduce-scatter.8
  572.1 44.5 reduce-scatter.10
  620.2 72.6 all-reduce.4
